TPU v7x, 32 devices: a whole 2x2x4 slice. The times are simulated.
32 devices in a mesh: row: 8 (over y, x, core), col: 4 (over z).
Axes of the slice: x: 2, y: 2, z: 4, core: 2. Of those that a mesh axis runs over, the one named last changes fastest.
Arguments:
- inputs_act: bfloat16 [1024, 4096], P('row', 'col'), may hold values from -6 to 6
- out_grad: bfloat16 [1024, 4096], P('row', 'col'), may hold values from -6 to 6
- pre_act: bfloat16 [1024, 16384], P('col', 'row'), may hold values from -8 to 8
- w_first: bfloat16 [4096, 16384], P('col', 'row'), may hold values from -0.046875 to 0.046875
- w_second: bfloat16 [16384, 4096], P('row', 'col'), may hold values from -0.09375 to 0.09375
Outputs:
- grad_input: bfloat16 [1024, 4096], P('row', 'col')
- grad_first: float32 [4096, 16384], P('col', 'row')
- grad_second: float32 [16384, 4096], P('row', 'col')
All inputs are finite; a program needn't handle non-finite values.
Results may differ from a plain program's by a relative error of at most 0.019.
Values may be sent and summed in bfloat16 or wider, within the bound.
A program may use at most 128 MiB of HBM per device.

v0:
```python
import math

import jax
import jax.numpy as jnp
from jax import lax
from jax.sharding import PartitionSpec as P

gelu_coef = 0.044715


def gelu_pair(pre_float):
    inner_c = math.sqrt(2.0 / math.pi)
    inner = inner_c * (pre_float + gelu_coef * pre_float * pre_float * pre_float)
    tanh_val = jnp.tanh(inner)
    act = 0.5 * pre_float * (1.0 + tanh_val)
    slope = 0.5 * (1.0 + tanh_val) + 0.5 * pre_float * (1.0 - tanh_val * tanh_val) * inner_c * (
        1.0 + 3.0 * gelu_coef * pre_float * pre_float
    )
    return (act, slope)


def contract_last(left, right):
    return lax.dot_general(
        left, right, (((1,), (1,)), ((), ())), preferred_element_type=jnp.float32
    )


def contract_first(left, right):
    return lax.dot_general(
        left, right, (((0,), (0,)), ((), ())), preferred_element_type=jnp.float32
    )


def on_device(inputs_act, out_grad, pre_act, w_first, w_second):
    total_tokens = pre_act.shape[0] * lax.axis_size("col")
    factor = 1.0 / math.sqrt(total_tokens)
    x_whole, dy_whole = (
        lax.all_gather(inputs_act, "row", axis=0, tiled=True),
        lax.all_gather(out_grad, "row", axis=0, tiled=True),
    )
    hidden_whole = lax.psum(contract_last(dy_whole, w_second).astype(jnp.bfloat16), "col").astype(
        jnp.float32
    )
    pre_whole = lax.all_gather(pre_act, "col", axis=0, tiled=True)
    act_float, slope = gelu_pair(pre_whole.astype(jnp.float32))
    act_whole = act_float.astype(jnp.bfloat16)
    grad_whole = (hidden_whole * slope).astype(jnp.bfloat16)
    grad_input = lax.psum_scatter(
        contract_last(grad_whole, w_first).astype(jnp.bfloat16),
        "row",
        scatter_dimension=0,
        tiled=True,
    )
    grad_first = contract_first(x_whole, grad_whole) * factor
    grad_second = contract_first(act_whole, dy_whole) * factor
    return (grad_input, grad_first, grad_second)


def solution(mesh):
    in_specs = (P("row", "col"), P("row", "col"), P("col", "row"), P("col", "row"), P("row", "col"))
    out_specs = (P("row", "col"), P("col", "row"), P("row", "col"))
    return jax.shard_map(
        on_device, mesh=mesh, in_specs=in_specs, out_specs=out_specs, check_vma=False
    )
```

profile of v0, /device:TPU:7, one launch (start us, length us, event | category | flops | bytes accessed | tf_op | source)
XLA Modules:
  0.0 357.6 jit_solution(10771306066762961557)
XLA Ops:
  7.2 0.0 all-gather.4.cloned.1.call-start
  7.2 0.7 all-gather.4.cloned.1.call-update
  7.9 0.0 all-gather.6.cloned.1.call-start
  7.9 0.7 all-gather.6.cloned.1.call-update
  8.6 0.0 all-reduce.2.cloned.1.call-start
  8.7 29.8 %all-gather.4.cloned.1.call-done = bf16[1024,1024]{1,0:T(8,128)(2,1)} async-done(((bf16[128,1024]{1,0:T(8,128)(2,1)}), bf16[1024,1024]{1,0:T(8,128)(2,1)}) %all-gather.4.cloned.1.call-update) | async-done | bytes 2097168 | tf_op jit(solution)/shard_map/all_gather | solution.py:39
  38.5 9.4 %convolution_convert_fusion = bf16[1024,2048]{1,0:T(8,128)(2,1)} fusion(bf16[1024,1024]{1,0:T(8,128)(2,1)} %all-gather.4.cloned.1.call-done, bf16[2048,1024]{1,0:T(8,128)(2,1)} %param.9), kind=kOutput, calls=%fused_computation.24 | convolution fusion | flops 4297064448 | bytes 10485760 | tf_op jit(solution)/shard_map/dot_general | solution.py:23
  47.9 0.0 all-reduce.2.cloned.1.call-update
  47.9 0.0 all-gather.8.cloned.1.call-start
  48.0 0.5 all-gather.8.cloned.1.call-update
  48.5 0.0 reduce-scatter.2.cloned.1.call-start
  48.5 72.8 %all-gather.6.cloned.1.call-done = bf16[1024,2048]{1,0:T(8,128)(2,1)} async-done(((bf16[256,2048]{1,0:T(8,128)(2,1)}), bf16[1024,2048]{1,0:T(8,128)(2,1)}) %all-gather.6.cloned.1.call-update) | async-done | bytes 4194320 | tf_op jit(solution)/shard_map/all_gather | solution.py:44
  121.4 156.5 %all-reduce.2.cloned.1.call-done = bf16[1024,2048]{1,0:T(8,128)(2,1)} async-done(((bf16[1024,2048]{1,0:T(8,128)(2,1)}), bf16[1024,2048]{1,0:T(8,128)(2,1)}) %all-reduce.2.cloned.1.call-update) | async-done | bytes 4194320 | tf_op jit(solution)/shard_map/psum | solution.py:41
  277.9 0.0 copy-start.1
  277.9 8.2 %fusion.6 = bf16[1024,2048]{1,0:T(8,128)(2,1)S(1)} fusion(bf16[1024,2048]{1,0:T(8,128)(2,1)} %all-gather.6.cloned.1.call-done, bf16[1024,2048]{1,0:T(8,128)(2,1)} %all-reduce.2.cloned.1.call-done), kind=kLoop, calls=%fused_computation.13 | loop fusion | flops 44040192 | bytes 12582912 | tf_op jit(solution)/shard_map/convert_element_type | solution.py:47
  286.1 0.0 copy-start
  286.1 2.0 copy-done
  288.1 0.0 copy-done.1
  288.1 0.0 copy-start.2
  288.1 5.7 %convolution_convert_fusion.1 = bf16[1024,1024]{1,0:T(8,128)(2,1)} fusion(bf16[1024,2048]{1,0:T(8,128)(2,1)S(1)} %fusion.6, bf16[1024,2048]{1,0:T(8,128)(2,1)S(1)} %copy-done.1), kind=kOutput, calls=%fused_computation.25 | convolution fusion | flops 4296015872 | bytes 10485760 | tf_op jit(solution)/shard_map/dot_general | solution.py:23
  293.9 0.0 reduce-scatter.2.cloned.1.call-update
  293.9 0.0 copy-done.2
  293.9 12.1 %convolution_multiply_fusion = f32[2048,1024]{1,0:T(8,128)} fusion(bf16[1024,1024]{1,0:T(8,128)(2,1)S(1)} %copy-done.2, bf16[1024,2048]{1,0:T(8,128)(2,1)} %all-gather.6.cloned.1.call-done), kind=kOutput, calls=%fused_computation.19 | convolution fusion | flops 4318035968 | bytes 14680064 | tf_op jit(solution)/shard_map/dot_general | solution.py:29
  305.9 0.3 all-gather.8.cloned.1.call-done
  306.2 10.6 %multiply_bitcast_fusion = f32[1024,2048]{0,1:T(8,128)} fusion(bf16[1024,2048]{1,0:T(8,128)(2,1)} %copy-done, bf16[1024,1024]{1,0:T(8,128)(2,1)} %all-gather.8.cloned.1.call-done), kind=kOutput, calls=%fused_computation.18 | convolution fusion | flops 4297064448 | bytes 14680064 | tf_op jit(solution)/shard_map/dot_general | solution.py:29
  316.9 9.3 %copy.8 = f32[1024,2048]{1,0:T(8,128)} copy(f32[1024,2048]{0,1:T(8,128)} %multiply_bitcast_fusion) | data formatting | bytes 16777216
  326.1 24.9 %reduce-scatter.2.cloned.1.call-done = bf16[128,1024]{1,0:T(8,128)(2,1)} async-done(((bf16[1024,1024]{1,0:T(8,128)(2,1)}), bf16[128,1024]{1,0:T(8,128)(2,1)}) %reduce-scatter.2.cloned.1.call-update) | async-done | bytes 262160 | tf_op jit(solution)/shard_map/reduce_scatter | solution.py:48
Async XLA Ops:
  7.2 31.3 %all-gather.4.cloned.1.call-start = ((), (), s32[]{:S(2)}) async-start(), calls=%async_computation.1 | async-start | bytes 2359296 | tf_op jit(solution)/shard_map/all_gather | solution.py:39
  7.9 113.5 %all-gather.6.cloned.1.call-start = ((), (), s32[]{:S(2)}) async-start(), calls=%async_computation.3 | async-start | bytes 5242880 | tf_op jit(solution)/shard_map/all_gather | solution.py:44
  8.6 269.2 %all-reduce.2.cloned.1.call-start = ((), (), s32[]{:S(2)}) async-start(), calls=%async_computation.2 | async-start | bytes 8388608 | tf_op jit(solution)/shard_map/psum | solution.py:41
  47.9 258.3 %all-gather.8.cloned.1.call-start = ((), (), s32[]{:S(2)}) async-start(), calls=%async_computation.5 | async-start | bytes 2359296 | tf_op jit(solution)/shard_map/all_gather | solution.py:38
  48.5 302.6 %reduce-scatter.2.cloned.1.call-start = ((), (), s32[]{:S(2)}) async-start(), calls=%async_computation.4 | async-start | bytes 2359296 | tf_op jit(solution)/shard_map/reduce_scatter | solution.py:48
  277.9 10.3 %copy-start.1 = (bf16[1024,2048]{1,0:T(8,128)(2,1)S(1)}, bf16[1024,2048]{1,0:T(8,128)(2,1)}, u32[]{:S(2)}) copy-start(bf16[1024,2048]{1,0:T(8,128)(2,1)} %param.8) | copy-start | bytes 12582916
  286.1 2.0 copy-start
  288.1 5.8 %copy-start.2 = (bf16[1024,1024]{1,0:T(8,128)(2,1)S(1)}, bf16[1024,1024]{1,0:T(8,128)(2,1)}, u32[]{:S(2)}) copy-start(bf16[1024,1024]{1,0:T(8,128)(2,1)} %all-gather.4.cloned.1.call-done) | copy-start | bytes 6291460
Sparse Core Ops, SparseCore 0:
  9.9 28.5 all-gather.3
  40.1 81.2 all-gather.5
  124.3 153.4 all-reduce.1
  279.8 26.4 all-gather.7
  310.3 40.7 reduce-scatter.1
where the time goes:
time: 360 us; the launch traced here: 358 us
  waiting for transfers between devices  286 us (79%)
  matrix products  37.8 us (10%)
  between operations  13.8 us (4%)
  local copies, waits for them, and re-layouts  11.3 us (3%)
  other arithmetic  8.23 us (2%)
    psum x1, waiting for transfers between devices, on_device(): lax.psum(contract_last(dy_whole, w_second).astype(jnp.bfloat16), 'col')  156 us
    all_gather x1, waiting for transfers between devices, on_device(): pre_whole = lax.all_gather(pre_act, 'col', axis=0, tiled=True)  72.8 us
    all_gather x1, waiting for transfers between devices, on_device(): lax.all_gather(out_grad, 'row', axis=0, tiled=True)  29.8 us
    reduce_scatter x1, waiting for transfers between devices, on_device(): lax.psum_scatter(contract_last(grad_whole, w_first).astype(jnp.bfloat16),...  24.9 us
    dot_general x2, matrix products, contract_first(): lax.dot_general(left, right, (((0,), (0,)), ((), ())), preferred_element_...  22.7 us
    dot_general x2, matrix products, contract_last(): lax.dot_general(left, right, (((1,), (1,)), ((), ())), preferred_element_...  15.1 us
    unnamed x7, local copies, waits for them, and re-layouts  11.3 us
    convert_element_type x1, other arithmetic, on_device(): grad_whole = (hidden_whole * slope).astype(jnp.bfloat16)  8.23 us
  transfers between devices with their start and end apart: 5, of which 5 were waited for; matrix products, arithmetic and copies ran while one was open for 15% of the time, Pallas kernels for 0%

commit v1 on v0

v1 whole, which is shorter than its diff:
```python
import functools
import math

import jax
import jax.numpy as jnp
from jax import lax
from jax.experimental import pallas as pl
from jax.experimental.pallas import tpu as pltpu
from jax.sharding import PartitionSpec as P

gelu_coef = 0.044715
inner_c = math.sqrt(2.0 / math.pi)
SUB = 2
STRIP = 16
MESH = pl.DeviceIdType.MESH


def tanh_of(p):
    return jnp.tanh(inner_c * (p + gelu_coef * p * p * p))


def act_of(p):
    return 0.5 * p * (1.0 + tanh_of(p))


def slope_of(p):
    t = tanh_of(p)
    return 0.5 * (1.0 + t) + 0.5 * p * (1.0 - t * t) * inner_c * (1.0 + 3.0 * gelu_coef * p * p)


def contract_last(left, right):
    return lax.dot_general(
        left, right, (((1,), (1,)), ((), ())), preferred_element_type=jnp.float32
    )


def contract_first(left, right):
    return lax.dot_general(
        left, right, (((0,), (0,)), ((), ())), preferred_element_type=jnp.float32
    )


def strips(first, count, body):
    def one(i, carry):
        body(pl.ds(pl.multiple_of(first + i * STRIP, STRIP), STRIP))
        return carry

    lax.fori_loop(0, count // STRIP, one, 0)


def kernel(
    R, N,
    x_ref, dy_ref, pre_ref, w1_ref, w2_ref,
    gi_out, x_out, dy_out, act_out, gp_out,
    w1, w2, dy, hid, pre, gp, act, slope, rs, gi_send, gi_recv, acc,
    loc, out_sem, dy_s, dy_r, x_s, x_r, pr_s, pr_r, rs_s, rs_r, gp_s, gp_r, gi_s, gi_r,
):
    r = lax.axis_index("row")
    c = lax.axis_index("col")
    q = R // N
    Tr = dy_ref.shape[0]
    Tc, H = pre_ref.shape
    Dc = dy_ref.shape[1]
    part = Tc // SUB
    last = N - 1
    f32, bf16 = jnp.float32, jnp.bfloat16

    barrier = pltpu.get_barrier_semaphore()
    for k in range(1, R):
        pl.semaphore_signal(barrier, inc=1, device_id={"row": lax.rem(r + k, R)}, device_id_type=MESH)

    @pl.when(c > 0)
    def _():
        pl.semaphore_signal(barrier, inc=1, device_id={"col": c - 1}, device_id_type=MESH)

    @pl.when(c < last)
    def _():
        pl.semaphore_signal(barrier, inc=1, device_id={"col": c + 1}, device_id_type=MESH)

    local = [
        pltpu.make_async_copy(dy_ref, dy.at[r], loc.at[0]),
        pltpu.make_async_copy(pre_ref, pre.at[c], loc.at[1]),
        pltpu.make_async_copy(w2_ref, w2, loc.at[2]),
        pltpu.make_async_copy(w1_ref, w1, loc.at[3]),
        pltpu.make_async_copy(x_ref, x_out.at[r], loc.at[4]),
    ]
    for copy in local:
        copy.start()
    ends = jnp.where(c > 0, 1, 0) + jnp.where(c < last, 1, 0)
    pl.semaphore_wait(barrier, R - 1 + ends)

    def row_send(src, dst, k, send, recv):
        return pltpu.make_async_remote_copy(
            src_ref=src, dst_ref=dst.at[r], send_sem=send.at[k], recv_sem=recv.at[r],
            device_id={"row": lax.rem(r + k, R)}, device_id_type=MESH)

    def row_recv(src, dst, k, send, recv):
        p = lax.rem(r + k, R)
        return pltpu.make_async_remote_copy(
            src_ref=src, dst_ref=dst.at[p], send_sem=send.at[k], recv_sem=recv.at[p],
            device_id={"row": p}, device_id_type=MESH)

    def sends_to(side):
        return c + 1 if side == 0 else c - 1

    def ag_shard(side, k):
        return c - k if side == 0 else c + k

    def ag_sends(side, k):
        return (c < last) & (c >= k) if side == 0 else (c > 0) & (c + k <= last)

    def ag_gets(side, k):
        return c >= k + 1 if side == 0 else c + 1 + k <= last

    def ag_got(side, k):
        return c - 1 - k if side == 0 else c + 1 + k

    def ag_copy(buf, shard, rows, side, send, recv, src=None):
        place = buf.at[shard] if rows is None else buf.at[shard, rows]
        return pltpu.make_async_remote_copy(
            src_ref=place if src is None else src, dst_ref=place, send_sem=send, recv_sem=recv,
            device_id={"col": sends_to(side)}, device_id_type=MESH)

    def rs_shard(side, k):
        return last - k + c if side == 0 else k - last + c

    def rs_sends(side, k):
        return c <= k if side == 0 else last - c <= k

    def rs_copy(side, k, j):
        rows = pl.ds(j * part, part)
        return pltpu.make_async_remote_copy(
            src_ref=hid.at[rs_shard(side, k), rows], dst_ref=rs.at[side, k, rows],
            send_sem=rs_s.at[side, k, j], recv_sem=rs_r.at[side, k, j],
            device_id={"col": sends_to(side)}, device_id_type=MESH)

    def rs_arrived(side, k, j):
        rows = pl.ds(j * part, part)
        return pltpu.make_async_remote_copy(
            src_ref=hid.at[c, rows], dst_ref=rs.at[side, k, rows],
            send_sem=rs_s.at[side, k, j], recv_sem=rs_r.at[side, k, j],
            device_id={"col": sends_to(side)}, device_id_type=MESH)

    def pre_step(k):
        for side in range(2):
            @pl.when(ag_sends(side, k))
            def _():
                if k > 0:
                    ag_copy(pre, ag_shard(side, k), None, side, pr_s.at[side, k - 1],
                            pr_r.at[side, k - 1]).wait_recv()
                ag_copy(pre, ag_shard(side, k), None, side, pr_s.at[side, k], pr_r.at[side, k],
                        pre_ref if k == 0 else None).start()

    for k in range(1, R):
        row_send(dy_ref, dy, k, dy_s, dy_r).start()
    pre_step(0)

    local[1].wait()

    def slope_strip(rows):
        slope[rows, :] = slope_of(pre[c, rows, :].astype(f32))

    strips(0, Tc, slope_strip)

    local[0].wait()
    local[2].wait()
    for k in range(1, R):
        row_recv(dy_ref, dy, k, dy_s, dy_r).wait_recv()
    for k in range(1, R):
        row_send(x_ref, x_out, k, x_s, x_r).start()

    tile_h = min(512, H)

    def partial(s):
        def one(i, carry):
            cols = pl.ds(pl.multiple_of(i * tile_h, tile_h), tile_h)
            left = dy[q * s : q * s + q].reshape(Tc, Dc)
            hid[s, :, cols] = contract_last(left, w2[cols, :]).astype(bf16)
            return carry

        lax.fori_loop(0, H // tile_h, one, 0)

    order = []
    for i in range((N + 1) // 2):
        order += [last - i] + ([i] if i != last - i else [])
    for s in order:
        partial(s)
        if s == last:
            @pl.when(c == 0)
            def _():
                for j in range(SUB):
                    rs_copy(0, 0, j).start()
        if s == 0:
            @pl.when(c == last)
            def _():
                for j in range(SUB):
                    rs_copy(1, 0, j).start()
    dy_copy = pltpu.make_async_copy(dy, dy_out, out_sem.at[0])
    dy_copy.start()

    pre_step(1)
    for k in range(1, last):
        for j in range(SUB):
            for side in range(2):
                edge = c == 0 if side == 0 else c == last

                @pl.when(rs_sends(side, k) & jnp.logical_not(edge))
                def _():
                    rs_arrived(side, k - 1, j).wait_recv()
                    s = rs_shard(side, k)

                    def add(rows):
                        total = hid[s, rows, :].astype(f32) + rs[side, k - 1, rows, :].astype(f32)
                        hid[s, rows, :] = total.astype(bf16)

                    strips(j * part, part, add)

                @pl.when(rs_sends(side, k))
                def _():
                    @pl.when(rs_sends(side, k - 1))
                    def _():
                        rs_copy(side, k - 1, j).wait_send()

                    rs_copy(side, k, j).start()
        if k + 1 < last:
            pre_step(k + 1)

    for j in range(SUB):
        rows_j = pl.ds(j * part, part)

        def load(rows):
            acc[rows, :] = hid[c, rows, :].astype(f32)

        strips(j * part, part, load)
        for side in range(2):
            @pl.when(c > 0 if side == 0 else c < last)
            def _():
                rs_arrived(side, last - 1, j).wait_recv()

                def add(rows):
                    acc[rows, :] = acc[rows, :] + rs[side, last - 1, rows, :].astype(f32)

                strips(j * part, part, add)

        def scale(rows):
            gp[c, rows, :] = (acc[rows, :] * slope[rows, :]).astype(bf16)

        strips(j * part, part, scale)
        for side in range(2):
            @pl.when(ag_sends(side, 0))
            def _():
                ag_copy(gp, c, rows_j, side, gp_s.at[side, 0, j], gp_r.at[side, 0, j]).start()

    local[3].wait()
    tile_d = min(512, Dc)

    def gi_copy(s, i):
        to = q * s + i
        return pltpu.make_async_remote_copy(
            src_ref=gi_send.at[s, pl.ds(i * Tr, Tr)], dst_ref=gi_recv.at[r],
            send_sem=gi_s.at[to], recv_sem=gi_r.at[r], device_id={"row": to}, device_id_type=MESH)

    def use_block(s):
        pltpu.make_async_copy(gp.at[s], gp_out.at[s], out_sem.at[1 + s]).start()

        def one(i, carry):
            cols = pl.ds(pl.multiple_of(i * tile_d, tile_d), tile_d)
            gi_send[s, :, cols] = contract_last(gp[s], w1[cols, :]).astype(bf16)
            return carry

        lax.fori_loop(0, Dc // tile_d, one, 0)
        for i in range(q):
            to = q * s + i

            @pl.when(to != r)
            def _():
                gi_copy(s, i).start()

            @pl.when(to == r)
            def _():
                gi_recv[r] = gi_send[s, pl.ds(i * Tr, Tr), :]

    def act_block(s):
        def one(rows):
            act[s, rows, :] = act_of(pre[s, rows, :].astype(f32)).astype(bf16)

        strips(0, Tc, one)
        pltpu.make_async_copy(act.at[s], act_out.at[s], out_sem.at[1 + N + s]).start()

    use_block(c)
    act_block(c)

    for k in range(last):
        for j in range(SUB):
            rows_j = pl.ds(j * part, part)
            for side in range(2):
                @pl.when(ag_gets(side, k))
                def _():
                    s = ag_got(side, k)
                    ag_copy(gp, s, rows_j, side, gp_s.at[side, k, j], gp_r.at[side, k, j]).wait_recv()
                    if k + 1 < last:
                        @pl.when(ag_sends(side, k + 1))
                        def _():
                            ag_copy(gp, s, rows_j, side, gp_s.at[side, k + 1, j],
                                    gp_r.at[side, k + 1, j]).start()
        for side in range(2):
            @pl.when(ag_gets(side, k))
            def _():
                s = ag_got(side, k)
                use_block(s)
                forwarded = ag_sends(side, k + 1) if k + 1 < last else c < 0

                @pl.when(jnp.logical_not(forwarded))
                def _():
                    ag_copy(pre, s, None, side, pr_s.at[side, k], pr_r.at[side, k]).wait_recv()

                act_block(s)

    for k in range(1, R):
        row_recv(gi_send.at[0, pl.ds(0, Tr)], gi_recv, k, gi_s, gi_r).wait_recv()

    def total_strip(rows):
        total = gi_recv[0, rows, :].astype(f32)
        for p in range(1, R):
            total = total + gi_recv[p, rows, :].astype(f32)
        gi_out[rows, :] = total.astype(bf16)

    strips(0, Tr, total_strip)

    for k in range(1, R):
        row_send(dy_ref, dy, k, dy_s, dy_r).wait_send()
        row_send(x_ref, x_out, k, x_s, x_r).wait_send()
        row_recv(x_ref, x_out, k, x_s, x_r).wait_recv()
    for s in range(N):
        for i in range(q):
            @pl.when(q * s + i != r)
            def _():
                gi_copy(s, i).wait_send()
        pltpu.make_async_copy(gp.at[s], gp_out.at[s], out_sem.at[1 + s]).wait()
        pltpu.make_async_copy(act.at[s], act_out.at[s], out_sem.at[1 + N + s]).wait()
    for side in range(2):
        for k in range(last):
            @pl.when(ag_sends(side, k))
            def _():
                s = ag_shard(side, k)
                ag_copy(pre, s, None, side, pr_s.at[side, k], pr_r.at[side, k],
                        pre_ref if k == 0 else None).wait_send()
                for j in range(SUB):
                    ag_copy(gp, s, pl.ds(j * part, part), side, gp_s.at[side, k, j],
                            gp_r.at[side, k, j]).wait_send()

        @pl.when(rs_sends(side, last - 1))
        def _():
            for j in range(SUB):
                rs_copy(side, last - 1, j).wait_send()
    dy_copy.wait()
    local[4].wait()


def exchange(R, N, x, dy, pre, w1, w2):
    Tr, Dc = dy.shape
    Tc, H = pre.shape
    bf16 = jnp.bfloat16
    dma = pltpu.SemaphoreType.DMA
    hbm = pl.BlockSpec(memory_space=pl.ANY)
    return pl.pallas_call(
        functools.partial(kernel, R, N),
        out_shape=[
            jax.ShapeDtypeStruct((Tr, Dc), bf16),
            jax.ShapeDtypeStruct((R, Tr, Dc), bf16),
            jax.ShapeDtypeStruct((R, Tr, Dc), bf16),
            jax.ShapeDtypeStruct((N, Tc, H), bf16),
            jax.ShapeDtypeStruct((N, Tc, H), bf16),
        ],
        in_specs=[hbm] * 5,
        out_specs=[pl.BlockSpec(memory_space=pltpu.VMEM)] + [hbm] * 4,
        scratch_shapes=[
            pltpu.VMEM(w1.shape, bf16),
            pltpu.VMEM(w2.shape, bf16),
            pltpu.VMEM((R, Tr, Dc), bf16),
            pltpu.VMEM((N, Tc, H), bf16),
            pltpu.VMEM((N, Tc, H), bf16),
            pltpu.VMEM((N, Tc, H), bf16),
            pltpu.VMEM((N, Tc, H), bf16),
            pltpu.VMEM((Tc, H), jnp.float32),
            pltpu.VMEM((2, N - 1, Tc, H), bf16),
            pltpu.VMEM((N, Tc, Dc), bf16),
            pltpu.VMEM((R, Tr, Dc), bf16),
            pltpu.VMEM((Tc, H), jnp.float32),
            dma((5,)),
            dma((1 + 2 * N,)),
            dma((R,)), dma((R,)), dma((R,)), dma((R,)),
            dma((2, N - 1)), dma((2, N - 1)),
            dma((2, N - 1, SUB)), dma((2, N - 1, SUB)),
            dma((2, N - 1, SUB)), dma((2, N - 1, SUB)),
            dma((R,)), dma((R,)),
        ],
        compiler_params=pltpu.CompilerParams(
            collective_id=0, has_side_effects=True, vmem_limit_bytes=56 * 2**20
        ),
    )(x, dy, pre, w1, w2)


def on_device(R, N, inputs_act, out_grad, pre_act, w_first, w_second):
    total_tokens = pre_act.shape[0] * N
    factor = 1.0 / math.sqrt(total_tokens)
    grad_input, x, dy, act, gp = exchange(R, N, inputs_act, out_grad, pre_act, w_first, w_second)
    x, dy = (a.reshape(total_tokens, -1) for a in (x, dy))
    act, gp = (a.reshape(total_tokens, -1) for a in (act, gp))
    grad_first = contract_first(x, gp) * factor
    grad_second = contract_first(act, dy) * factor
    return (grad_input, grad_first, grad_second)


def solution(mesh):
    in_specs = (P("row", "col"), P("row", "col"), P("col", "row"), P("col", "row"), P("row", "col"))
    out_specs = (P("row", "col"), P("col", "row"), P("row", "col"))
    return jax.shard_map(
        functools.partial(on_device, mesh.shape["row"], mesh.shape["col"]),
        mesh=mesh, in_specs=in_specs, out_specs=out_specs, check_vma=False,
    )
```

time: 360 us -> 209 us (0.58)
  waiting for transfers between devices: 286 us -> 0 us
  Pallas kernels: 0 us -> 188 us
  matrix products: 37.8 us -> 17.8 us
  between operations: 13.8 us -> 0.66 us
  local copies, waits for them, and re-layouts: 11.3 us -> 0.71 us
  other arithmetic: 8.23 us -> 0 us
    pallas_call x0 -> x1, Pallas kernels: none -> 188 us  [exchange(): pl.pallas_call(functools.partial(kernel, R, N), out_shape=[jax.ShapeDtype...]
    psum x1 -> x0, waiting for transfers between devices: 156 us -> none  [on_device(): lax.psum(contract_last(dy_whole, w_second).astype(jnp.bfloat16), 'col')]
    all_gather x3 -> x0, waiting for transfers between devices: 103 us -> none  [the longest x1 72.8 us: on_device(): pre_whole = lax.all_gather(pre_act, 'col', axis=0, tiled=True)]
    reduce_scatter x1 -> x0, waiting for transfers between devices: 24.9 us -> none  [on_device(): lax.psum_scatter(contract_last(grad_whole, w_first).astype(jnp.bfloat16),...]
    dot_general x2 -> x0, matrix products: 15.1 us -> none  [contract_last(): lax.dot_general(left, right, (((1,), (1,)), ((), ())), preferred_element_...]
    unnamed x7, local copies, waits for them, and re-layouts: 11.3 us -> 0.71 us
    convert_element_type x1 -> x0, other arithmetic: 8.23 us -> none  [on_device(): grad_whole = (hidden_whole * slope).astype(jnp.bfloat16)]
    dot_general x2, matrix products: 22.7 us -> 17.8 us  [contract_first(): lax.dot_general(left, right, (((0,), (0,)), ((), ())), preferred_element_...]
  transfers between devices with their start and end apart: 5 -> 0, of which waited for: 5 -> 0; matrix products, arithmetic and copies ran while one was open for 15% -> 0% of each run, Pallas kernels for 0% -> 0%
where the time goes in v1:
time: 209 us; the launch traced here: 207 us
  Pallas kernels  188 us (90%)
  matrix products  17.8 us (9%)
    pallas_call x1, Pallas kernels, exchange(): pl.pallas_call(functools.partial(kernel, R, N), out_shape=[jax.ShapeDtype...  188 us
    dot_general x2, matrix products, contract_first(): lax.dot_general(left, right, (((0,), (0,)), ((), ())), preferred_element_...  17.8 us

profile of v1, /device:TPU:7, one launch (start us, length us, event | category | flops | bytes accessed | tf_op | source)
XLA Modules:
  0.0 207.5 jit_solution(11477966849581974440)
XLA Ops:
  0.6 188.3 %shard_map.76 = (bf16[128,1024]{1,0:T(8,128)(2,1)}, bf16[8,128,1024]{2,1,0:T(8,128)(2,1)}, bf16[8,128,1024]{2,1,0:T(8,128)(2,1)}, bf16[4,256,2048]{2,1,0:T(8,128)(2,1)}, bf16[4,256,2048]{2,1,0:T(8,128)(2,1)}) custom-call(bf16[128,1024]{1,0:T(8,128)(2,1)} %x_ref.1, bf16[128,1024]{1,0:T(8,128)(2,1)} %dy_ref.1, bf16[256,2048]{1,0:T(8,128)(2,1)} %pre_ref.1, ...), custom_call_target="tpu_custom_call" | custom-call | tf_op jit(solution)/shard_map/pallas_call | solution.py:366
  188.9 0.0 copy-start.1
  189.0 0.0 copy-start.2
  189.0 10.9 %convolution_multiply_fusion.1 = f32[1024,2048]{1,0:T(8,128)} fusion(bf16[1024,1024]{1,0:T(8,128)(2,1)} %bitcast.11, bf16[1024,2048]{1,0:T(8,128)(2,1)} %bitcast.9), kind=kOutput, calls=%fused_computation.1 | convolution fusion | flops 4297064448 | bytes 14680064 | tf_op jit(solution)/shard_map/dot_general | solution.py:38
  199.9 0.0 copy-done.1
  199.9 0.0 copy-done.2
  199.9 0.0 copy-start
  199.9 6.8 %convolution_multiply_fusion = f32[2048,1024]{1,0:T(8,128)} fusion(bf16[1024,2048]{1,0:T(8,128)(2,1)S(1)} %bitcast.8, bf16[1024,1024]{1,0:T(8,128)(2,1)S(1)} %bitcast.10), kind=kOutput, calls=%fused_computation | convolution fusion | flops 4297064448 | bytes 14680064 | tf_op jit(solution)/shard_map/dot_general | solution.py:38
  206.7 0.0 copy-done
  206.7 0.7 copy.9
Async XLA Ops:
  188.9 11.0 %copy-start.1 = (bf16[4,256,2048]{2,1,0:T(8,128)(2,1)S(1)}, bf16[4,256,2048]{2,1,0:T(8,128)(2,1)}, u32[]{:S(2)}) copy-start(bf16[4,256,2048]{2,1,0:T(8,128)(2,1)} %get-tuple-element.11) | copy-start | bytes 12582916
  189.0 11.0 %copy-start.2 = (bf16[8,128,1024]{2,1,0:T(8,128)(2,1)S(1)}, bf16[8,128,1024]{2,1,0:T(8,128)(2,1)}, u32[]{:S(2)}) copy-start(bf16[8,128,1024]{2,1,0:T(8,128)(2,1)} %get-tuple-element.12) | copy-start | bytes 6291460
  199.9 6.8 %copy-start = (bf16[128,1024]{1,0:T(8,128)(2,1)S(1)}, bf16[128,1024]{1,0:T(8,128)(2,1)}, u32[]{:S(2)}) copy-start(bf16[128,1024]{1,0:T(8,128)(2,1)} %get-tuple-element.16) | copy-start | bytes 786436

commit v2 on v1

--- a/solution.py
+++ b/solution.py
@@ -51,9 +51,9 @@
 def kernel(
     R, N,
     x_ref, dy_ref, pre_ref, w1_ref, w2_ref,
-    gi_out, x_out, dy_out, act_out, gp_out,
-    w1, w2, dy, hid, pre, gp, act, slope, rs, gi_send, gi_recv, acc,
-    loc, out_sem, dy_s, dy_r, x_s, x_r, pr_s, pr_r, rs_s, rs_r, gp_s, gp_r, gi_s, gi_r,
+    gi_out, gs_out, gf_out, xf_out, gpf_out,
+    w1, w2, dy, x, hid, pre, gp, act, slope, rs, gi_send, gi_recv, acc, gf,
+    loc, out_sem, dy_s, dy_r, x_s, x_r, fw_s, pr_s, pr_r, rs_s, rs_r, gp_s, gp_r, gi_s, gi_r,
 ):
     r = lax.axis_index("row")
     c = lax.axis_index("col")
@@ -82,23 +82,51 @@
         pltpu.make_async_copy(pre_ref, pre.at[c], loc.at[1]),
         pltpu.make_async_copy(w2_ref, w2, loc.at[2]),
         pltpu.make_async_copy(w1_ref, w1, loc.at[3]),
-        pltpu.make_async_copy(x_ref, x_out.at[r], loc.at[4]),
+        pltpu.make_async_copy(x_ref, x.at[r], loc.at[4]),
     ]
     for copy in local:
         copy.start()
     ends = jnp.where(c > 0, 1, 0) + jnp.where(c < last, 1, 0)
     pl.semaphore_wait(barrier, R - 1 + ends)
 
+    sibling = r + 1 - 2 * lax.rem(r, 2)
+    chips = R // 2
+
     def row_send(src, dst, k, send, recv):
+        to = sibling if k == 0 else lax.rem(r + 2 * k, R)
         return pltpu.make_async_remote_copy(
             src_ref=src, dst_ref=dst.at[r], send_sem=send.at[k], recv_sem=recv.at[r],
-            device_id={"row": lax.rem(r + k, R)}, device_id_type=MESH)
-
-    def row_recv(src, dst, k, send, recv):
-        p = lax.rem(r + k, R)
-        return pltpu.make_async_remote_copy(
-            src_ref=src, dst_ref=dst.at[p], send_sem=send.at[k], recv_sem=recv.at[p],
-            device_id={"row": p}, device_id_type=MESH)
+            device_id={"row": to}, device_id_type=MESH)
+
+    def row_got(src, dst, p, send, recv):
+        return pltpu.make_async_remote_copy(
+            src_ref=src, dst_ref=dst.at[p], send_sem=send, recv_sem=recv.at[p],
+            device_id={"row": sibling}, device_id_type=MESH)
+
+    def row_forward(which, dst, k, recv):
+        p = lax.rem(r + 2 * k, R)
+        return pltpu.make_async_remote_copy(
+            src_ref=dst.at[p], dst_ref=dst.at[p], send_sem=fw_s.at[which, k], recv_sem=recv.at[p],
+            device_id={"row": sibling}, device_id_type=MESH)
+
+    def row_start(src, dst, send, recv):
+        for k in list(range(1, chips)) + [0]:
+            row_send(src, dst, k, send, recv).start()
+
+    def row_pass(which, src, dst, send, recv):
+        for k in range(1, chips):
+            row_got(src, dst, lax.rem(r + 2 * k, R), send.at[k], recv).wait_recv()
+            row_forward(which, dst, k, recv).start()
+
+    def row_rest(src, dst, send, recv):
+        for k in range(chips):
+            row_got(src, dst, lax.rem(sibling + 2 * k, R), send.at[k], recv).wait_recv()
+
+    def row_end(which, src, dst, send, recv):
+        for k in range(chips):
+            row_send(src, dst, k, send, recv).wait_send()
+            if k > 0:
+                row_forward(which, dst, k, recv).wait_send()
 
     def sends_to(side):
         return c + 1 if side == 0 else c - 1
@@ -151,8 +179,7 @@
                 ag_copy(pre, ag_shard(side, k), None, side, pr_s.at[side, k], pr_r.at[side, k],
                         pre_ref if k == 0 else None).start()
 
-    for k in range(1, R):
-        row_send(dy_ref, dy, k, dy_s, dy_r).start()
+    row_start(dy_ref, dy, dy_s, dy_r)
     pre_step(0)
 
     local[1].wait()
@@ -164,10 +191,9 @@
 
     local[0].wait()
     local[2].wait()
-    for k in range(1, R):
-        row_recv(dy_ref, dy, k, dy_s, dy_r).wait_recv()
-    for k in range(1, R):
-        row_send(x_ref, x_out, k, x_s, x_r).start()
+    row_pass(0, dy_ref, dy, dy_s, dy_r)
+    row_rest(dy_ref, dy, dy_s, dy_r)
+    row_start(x_ref, x, x_s, x_r)
 
     tile_h = min(512, H)
 
@@ -195,10 +221,28 @@
             def _():
                 for j in range(SUB):
                     rs_copy(1, 0, j).start()
-    dy_copy = pltpu.make_async_copy(dy, dy_out, out_sem.at[0])
-    dy_copy.start()
+
+    def act_block(s):
+        def one(rows):
+            act[s, rows, :] = act_of(pre[s, rows, :].astype(f32)).astype(bf16)
+
+        strips(0, Tc, one)
+
+    def act_step(k):
+        for side in range(2):
+            @pl.when(ag_gets(side, k))
+            def _():
+                s = ag_got(side, k)
+                forwarded = ag_sends(side, k + 1) if k + 1 < last else c < 0
+
+                @pl.when(jnp.logical_not(forwarded))
+                def _():
+                    ag_copy(pre, s, None, side, pr_s.at[side, k], pr_r.at[side, k]).wait_recv()
+
+                act_block(s)
 
     pre_step(1)
+    act_block(c)
     for k in range(1, last):
         for j in range(SUB):
             for side in range(2):
@@ -224,6 +268,9 @@
                     rs_copy(side, k, j).start()
         if k + 1 < last:
             pre_step(k + 1)
+        if k == 1:
+            row_pass(1, x_ref, x, x_s, x_r)
+        act_step(k - 1)
 
     for j in range(SUB):
         rows_j = pl.ds(j * part, part)
@@ -261,8 +308,6 @@
             send_sem=gi_s.at[to], recv_sem=gi_r.at[r], device_id={"row": to}, device_id_type=MESH)
 
     def use_block(s):
-        pltpu.make_async_copy(gp.at[s], gp_out.at[s], out_sem.at[1 + s]).start()
-
         def one(i, carry):
             cols = pl.ds(pl.multiple_of(i * tile_d, tile_d), tile_d)
             gi_send[s, :, cols] = contract_last(gp[s], w1[cols, :]).astype(bf16)
@@ -280,15 +325,39 @@
             def _():
                 gi_recv[r] = gi_send[s, pl.ds(i * Tr, Tr), :]
 
-    def act_block(s):
-        def one(rows):
-            act[s, rows, :] = act_of(pre[s, rows, :].astype(f32)).astype(bf16)
-
-        strips(0, Tc, one)
-        pltpu.make_async_copy(act.at[s], act_out.at[s], out_sem.at[1 + N + s]).start()
-
+    far = jnp.where(c < N // 2, last, 0)
+
+    def gf_block(s, first):
+        left = x[pl.ds(q * s, q)].reshape(Tc, Dc)
+
+        def one(i, carry):
+            cols = pl.ds(pl.multiple_of(i * tile_h, tile_h), tile_h)
+            term = contract_first(left, gp[s, :, cols])
+            gf[:, cols] = term if first else gf[:, cols] + term
+            return carry
+
+        lax.fori_loop(0, H // tile_h, one, 0)
+
+    def gs_all():
+        def one(i, carry):
+            rows = pl.ds(pl.multiple_of(i * tile_g, tile_g), tile_g)
+            left = act[:, :, rows].reshape(N * Tc, tile_g)
+            w2[rows, :] = contract_first(left, dy[...].reshape(N * Tc, Dc)).astype(bf16)
+            return carry
+
+        lax.fori_loop(0, H // tile_g, one, 0)
+
+    tile_g = min(256, H)
+    gs_copy = pltpu.make_async_copy(w2, gs_out, out_sem.at[0])
+    gf_copy = pltpu.make_async_copy(gf, gf_out, out_sem.at[1])
+    xf_copy = pltpu.make_async_copy(x.at[pl.ds(q * far, q)], xf_out, out_sem.at[2])
+    gpf_copy = pltpu.make_async_copy(gp.at[far], gpf_out, out_sem.at[3])
     use_block(c)
-    act_block(c)
+    act_step(last - 1)
+    local[4].wait()
+    row_rest(x_ref, x, x_s, x_r)
+    xf_copy.start()
+    gf_block(c, True)
 
     for k in range(last):
         for j in range(SUB):
@@ -308,16 +377,24 @@
             def _():
                 s = ag_got(side, k)
                 use_block(s)
-                forwarded = ag_sends(side, k + 1) if k + 1 < last else c < 0
-
-                @pl.when(jnp.logical_not(forwarded))
+
+                @pl.when(s == far)
                 def _():
-                    ag_copy(pre, s, None, side, pr_s.at[side, k], pr_r.at[side, k]).wait_recv()
-
-                act_block(s)
+                    gpf_copy.start()
+
+                if k + 1 < last:
+                    @pl.when(s != far)
+                    def _():
+                        gf_block(s, False)
+        if k == 0:
+            gs_all()
+            gs_copy.start()
+        if k == last - 2:
+            gf_copy.start()
 
     for k in range(1, R):
-        row_recv(gi_send.at[0, pl.ds(0, Tr)], gi_recv, k, gi_s, gi_r).wait_recv()
+        p = lax.rem(r + k, R)
+        row_got(gi_send.at[0, pl.ds(0, Tr)], gi_recv, p, gi_s.at[p], gi_r).wait_recv()
 
     def total_strip(rows):
         total = gi_recv[0, rows, :].astype(f32)
@@ -327,17 +404,13 @@
 
     strips(0, Tr, total_strip)
 
-    for k in range(1, R):
-        row_send(dy_ref, dy, k, dy_s, dy_r).wait_send()
-        row_send(x_ref, x_out, k, x_s, x_r).wait_send()
-        row_recv(x_ref, x_out, k, x_s, x_r).wait_recv()
+    row_end(0, dy_ref, dy, dy_s, dy_r)
+    row_end(1, x_ref, x, x_s, x_r)
     for s in range(N):
         for i in range(q):
             @pl.when(q * s + i != r)
             def _():
                 gi_copy(s, i).wait_send()
-        pltpu.make_async_copy(gp.at[s], gp_out.at[s], out_sem.at[1 + s]).wait()
-        pltpu.make_async_copy(act.at[s], act_out.at[s], out_sem.at[1 + N + s]).wait()
     for side in range(2):
         for k in range(last):
             @pl.when(ag_sends(side, k))
@@ -353,8 +426,8 @@
         def _():
             for j in range(SUB):
                 rs_copy(side, last - 1, j).wait_send()
-    dy_copy.wait()
-    local[4].wait()
+    for copy in (gs_copy, gf_copy, xf_copy, gpf_copy):
+        copy.wait()
 
 
 def exchange(R, N, x, dy, pre, w1, w2):
@@ -367,16 +440,17 @@
         functools.partial(kernel, R, N),
         out_shape=[
             jax.ShapeDtypeStruct((Tr, Dc), bf16),
-            jax.ShapeDtypeStruct((R, Tr, Dc), bf16),
-            jax.ShapeDtypeStruct((R, Tr, Dc), bf16),
-            jax.ShapeDtypeStruct((N, Tc, H), bf16),
-            jax.ShapeDtypeStruct((N, Tc, H), bf16),
+            jax.ShapeDtypeStruct((H, Dc), bf16),
+            jax.ShapeDtypeStruct((Dc, H), jnp.float32),
+            jax.ShapeDtypeStruct((R // N, Tr, Dc), bf16),
+            jax.ShapeDtypeStruct((Tc, H), bf16),
         ],
         in_specs=[hbm] * 5,
         out_specs=[pl.BlockSpec(memory_space=pltpu.VMEM)] + [hbm] * 4,
         scratch_shapes=[
             pltpu.VMEM(w1.shape, bf16),
             pltpu.VMEM(w2.shape, bf16),
+            pltpu.VMEM((R, Tr, Dc), bf16),
             pltpu.VMEM((R, Tr, Dc), bf16),
             pltpu.VMEM((N, Tc, H), bf16),
             pltpu.VMEM((N, Tc, H), bf16),
@@ -387,16 +461,17 @@
             pltpu.VMEM((N, Tc, Dc), bf16),
             pltpu.VMEM((R, Tr, Dc), bf16),
             pltpu.VMEM((Tc, H), jnp.float32),
+            pltpu.VMEM((Dc, H), jnp.float32),
             dma((5,)),
-            dma((1 + 2 * N,)),
-            dma((R,)), dma((R,)), dma((R,)), dma((R,)),
+            dma((4,)),
+            dma((R // 2,)), dma((R,)), dma((R // 2,)), dma((R,)), dma((2, R // 2)),
             dma((2, N - 1)), dma((2, N - 1)),
             dma((2, N - 1, SUB)), dma((2, N - 1, SUB)),
             dma((2, N - 1, SUB)), dma((2, N - 1, SUB)),
             dma((R,)), dma((R,)),
         ],
         compiler_params=pltpu.CompilerParams(
-            collective_id=0, has_side_effects=True, vmem_limit_bytes=56 * 2**20
+            collective_id=0, has_side_effects=True, vmem_limit_bytes=60 * 2**20
         ),
     )(x, dy, pre, w1, w2)
 
@@ -404,11 +479,12 @@
 def on_device(R, N, inputs_act, out_grad, pre_act, w_first, w_second):
     total_tokens = pre_act.shape[0] * N
     factor = 1.0 / math.sqrt(total_tokens)
-    grad_input, x, dy, act, gp = exchange(R, N, inputs_act, out_grad, pre_act, w_first, w_second)
-    x, dy = (a.reshape(total_tokens, -1) for a in (x, dy))
-    act, gp = (a.reshape(total_tokens, -1) for a in (act, gp))
-    grad_first = contract_first(x, gp) * factor
-    grad_second = contract_first(act, dy) * factor
+    grad_input, gs, gf, x_far, gp_far = exchange(
+        R, N, inputs_act, out_grad, pre_act, w_first, w_second
+    )
+    x_far = x_far.reshape(gp_far.shape[0], -1)
+    grad_first = (gf + contract_first(x_far, gp_far)) * factor
+    grad_second = gs.astype(jnp.float32) * factor
     return (grad_input, grad_first, grad_second)
 
 

time: 209 us -> 203 us (0.971)
  matrix products: 17.8 us -> 8.7 us
  other arithmetic: 0 us -> 4.59 us
    dot_general x2 -> x1, matrix products: 17.8 us -> 8.7 us  [contract_first(): lax.dot_general(left, right, (((0,), (0,)), ((), ())), preferred_element_...]
    mul x0 -> x1, other arithmetic: none -> 4.59 us  [on_device(): grad_second = gs.astype(jnp.float32) * factor]
where the time goes in v2:
time: 203 us
  Pallas kernels  188 us (93%)
  matrix products  8.7 us (4%)
  other arithmetic  4.59 us (2%)
    pallas_call x1, Pallas kernels, exchange(): pl.pallas_call(functools.partial(kernel, R, N), out_shape=[jax.ShapeDtype...  188 us
    dot_general x1, matrix products, contract_first(): lax.dot_general(left, right, (((0,), (0,)), ((), ())), preferred_element_...  8.7 us
    mul x1, other arithmetic, on_device(): grad_second = gs.astype(jnp.float32) * factor  4.59 us

profile of v2, /device:TPU:7, one launch (start us, length us, event | category | flops | bytes accessed | tf_op | source)
XLA Modules:
  0.0 203.0 jit_solution(16301887727579425115)
XLA Ops:
  0.6 188.4 %shard_map.76 = (bf16[128,1024]{1,0:T(8,128)(2,1)}, bf16[2048,1024]{1,0:T(8,128)(2,1)}, f32[1024,2048]{1,0:T(8,128)}, bf16[2,128,1024]{2,1,0:T(8,128)(2,1)}, bf16[256,2048]{1,0:T(8,128)(2,1)}) custom-call(bf16[128,1024]{1,0:T(8,128)(2,1)} %x_ref.1, bf16[128,1024]{1,0:T(8,128)(2,1)} %dy_ref.1, bf16[256,2048]{1,0:T(8,128)(2,1)} %pre_ref.1, ...), custom_call_target="tpu_custom_call" | custom-call | tf_op jit(solution)/shard_map/pallas_call | solution.py:439
  189.0 0.0 copy-start
  189.0 8.7 %add_multiply_fusion = f32[1024,2048]{1,0:T(8,128)} fusion(f32[1024,2048]{1,0:T(8,128)} %get-tuple-element.9, bf16[256,1024]{1,0:T(8,128)(2,1)} %bitcast.3, bf16[256,2048]{1,0:T(8,128)(2,1)} %get-tuple-element.11), kind=kOutput, calls=%fused_computation.1 | convolution fusion | flops 1077936128 | bytes 18350080 | tf_op jit(solution)/shard_map/dot_general | solution.py:38
  197.7 0.0 copy-done
  197.8 0.0 copy-start.1
  197.8 4.6 %convert_multiply_fusion = f32[2048,1024]{1,0:T(8,128)} fusion(bf16[2048,1024]{1,0:T(8,128)(2,1)S(1)} %copy-done), kind=kLoop, calls=%fused_computation | loop fusion | flops 4194304 | bytes 12582912 | tf_op jit(solution)/shard_map/mul | solution.py:487
  202.3 0.0 copy-done.1
  202.3 0.7 copy.9
Async XLA Ops:
  189.0 8.7 %copy-start = (bf16[2048,1024]{1,0:T(8,128)(2,1)S(1)}, bf16[2048,1024]{1,0:T(8,128)(2,1)}, u32[]{:S(2)}) copy-start(bf16[2048,1024]{1,0:T(8,128)(2,1)} %get-tuple-element.12) | copy-start | bytes 12582916
  197.8 4.6 %copy-start.1 = (bf16[128,1024]{1,0:T(8,128)(2,1)S(1)}, bf16[128,1024]{1,0:T(8,128)(2,1)}, u32[]{:S(2)}) copy-start(bf16[128,1024]{1,0:T(8,128)(2,1)} %get-tuple-element.16) | copy-start | bytes 786436

commit v3 on v2

--- a/solution.py
+++ b/solution.py
@@ -10,7 +10,6 @@
 
 gelu_coef = 0.044715
 inner_c = math.sqrt(2.0 / math.pi)
-SUB = 2
 STRIP = 16
 MESH = pl.DeviceIdType.MESH
 
@@ -51,13 +50,13 @@
 def kernel(
     R, N,
     x_ref, dy_ref, pre_ref, w1_ref, w2_ref,
-    gi_out, gs_out, gf_out, xf_out, gpf_out,
-    w1, w2, dy, x, hid, pre, gp, act, slope, rs, gi_send, gi_recv, acc, gf,
+    gi_out, gs_out, gf_out,
+    w1, w2, dy, x, hid, pre, gp, act, slope, rs, gi_send, gi_recv, acc, gf, gf_half,
     loc, out_sem, dy_s, dy_r, x_s, x_r, fw_s, pr_s, pr_r, rs_s, rs_r, gp_s, gp_r, gi_s, gi_r,
 ):
     r = lax.axis_index("row")
     c = lax.axis_index("col")
-    q = R // N
+    q = SUB = R // N
     Tr = dy_ref.shape[0]
     Tc, H = pre_ref.shape
     Dc = dy_ref.shape[1]
@@ -307,33 +306,37 @@
             src_ref=gi_send.at[s, pl.ds(i * Tr, Tr)], dst_ref=gi_recv.at[r],
             send_sem=gi_s.at[to], recv_sem=gi_r.at[r], device_id={"row": to}, device_id_type=MESH)
 
-    def use_block(s):
-        def one(i, carry):
-            cols = pl.ds(pl.multiple_of(i * tile_d, tile_d), tile_d)
-            gi_send[s, :, cols] = contract_last(gp[s], w1[cols, :]).astype(bf16)
+    def use_piece(s, i):
+        rows = pl.ds(i * Tr, Tr)
+
+        def one(t, carry):
+            cols = pl.ds(pl.multiple_of(t * tile_d, tile_d), tile_d)
+            gi_send[s, rows, cols] = contract_last(gp[s, rows, :], w1[cols, :]).astype(bf16)
             return carry
 
         lax.fori_loop(0, Dc // tile_d, one, 0)
-        for i in range(q):
-            to = q * s + i
-
-            @pl.when(to != r)
-            def _():
-                gi_copy(s, i).start()
-
-            @pl.when(to == r)
-            def _():
-                gi_recv[r] = gi_send[s, pl.ds(i * Tr, Tr), :]
+        to = q * s + i
+
+        @pl.when(to != r)
+        def _():
+            gi_copy(s, i).start()
+
+        @pl.when(to == r)
+        def _():
+            gi_recv[r] = gi_send[s, rows, :]
 
     far = jnp.where(c < N // 2, last, 0)
 
-    def gf_block(s, first):
+    def gf_block(s, first, end=False):
         left = x[pl.ds(q * s, q)].reshape(Tc, Dc)
 
         def one(i, carry):
             cols = pl.ds(pl.multiple_of(i * tile_h, tile_h), tile_h)
             term = contract_first(left, gp[s, :, cols])
-            gf[:, cols] = term if first else gf[:, cols] + term
+            if end:
+                gf_half[:, cols] = (gf[:, cols] + term).astype(bf16)
+            else:
+                gf[:, cols] = term if first else gf[:, cols] + term
             return carry
 
         lax.fori_loop(0, H // tile_h, one, 0)
@@ -349,14 +352,12 @@
 
     tile_g = min(256, H)
     gs_copy = pltpu.make_async_copy(w2, gs_out, out_sem.at[0])
-    gf_copy = pltpu.make_async_copy(gf, gf_out, out_sem.at[1])
-    xf_copy = pltpu.make_async_copy(x.at[pl.ds(q * far, q)], xf_out, out_sem.at[2])
-    gpf_copy = pltpu.make_async_copy(gp.at[far], gpf_out, out_sem.at[3])
-    use_block(c)
+    gf_copy = pltpu.make_async_copy(gf_half, gf_out, out_sem.at[1])
+    for i in range(q):
+        use_piece(c, i)
     act_step(last - 1)
     local[4].wait()
     row_rest(x_ref, x, x_s, x_r)
-    xf_copy.start()
     gf_block(c, True)
 
     for k in range(last):
@@ -372,25 +373,22 @@
                         def _():
                             ag_copy(gp, s, rows_j, side, gp_s.at[side, k + 1, j],
                                     gp_r.at[side, k + 1, j]).start()
-        for side in range(2):
-            @pl.when(ag_gets(side, k))
-            def _():
+            for side in range(2):
+                @pl.when(ag_gets(side, k))
+                def _():
+                    use_piece(ag_got(side, k), j)
+        if k + 1 < last:
+            for side in range(2):
                 s = ag_got(side, k)
-                use_block(s)
-
-                @pl.when(s == far)
-                def _():
-                    gpf_copy.start()
-
-                if k + 1 < last:
-                    @pl.when(s != far)
-                    def _():
-                        gf_block(s, False)
+
+                @pl.when(ag_gets(side, k) & (s != far))
+                def _():
+                    gf_block(s, False)
         if k == 0:
             gs_all()
             gs_copy.start()
-        if k == last - 2:
-            gf_copy.start()
+    gf_block(far, False, True)
+    gf_copy.start()
 
     for k in range(1, R):
         p = lax.rem(r + k, R)
@@ -426,13 +424,14 @@
         def _():
             for j in range(SUB):
                 rs_copy(side, last - 1, j).wait_send()
-    for copy in (gs_copy, gf_copy, xf_copy, gpf_copy):
+    for copy in (gs_copy, gf_copy):
         copy.wait()
 
 
 def exchange(R, N, x, dy, pre, w1, w2):
     Tr, Dc = dy.shape
     Tc, H = pre.shape
+    SUB = R // N
     bf16 = jnp.bfloat16
     dma = pltpu.SemaphoreType.DMA
     hbm = pl.BlockSpec(memory_space=pl.ANY)
@@ -441,12 +440,10 @@
         out_shape=[
             jax.ShapeDtypeStruct((Tr, Dc), bf16),
             jax.ShapeDtypeStruct((H, Dc), bf16),
-            jax.ShapeDtypeStruct((Dc, H), jnp.float32),
-            jax.ShapeDtypeStruct((R // N, Tr, Dc), bf16),
-            jax.ShapeDtypeStruct((Tc, H), bf16),
+            jax.ShapeDtypeStruct((Dc, H), bf16),
         ],
         in_specs=[hbm] * 5,
-        out_specs=[pl.BlockSpec(memory_space=pltpu.VMEM)] + [hbm] * 4,
+        out_specs=[pl.BlockSpec(memory_space=pltpu.VMEM)] + [hbm] * 2,
         scratch_shapes=[
             pltpu.VMEM(w1.shape, bf16),
             pltpu.VMEM(w2.shape, bf16),
@@ -462,8 +459,9 @@
             pltpu.VMEM((R, Tr, Dc), bf16),
             pltpu.VMEM((Tc, H), jnp.float32),
             pltpu.VMEM((Dc, H), jnp.float32),
+            pltpu.VMEM((Dc, H), bf16),
             dma((5,)),
-            dma((4,)),
+            dma((2,)),
             dma((R // 2,)), dma((R,)), dma((R // 2,)), dma((R,)), dma((2, R // 2)),
             dma((2, N - 1)), dma((2, N - 1)),
             dma((2, N - 1, SUB)), dma((2, N - 1, SUB)),
@@ -479,11 +477,8 @@
 def on_device(R, N, inputs_act, out_grad, pre_act, w_first, w_second):
     total_tokens = pre_act.shape[0] * N
     factor = 1.0 / math.sqrt(total_tokens)
-    grad_input, gs, gf, x_far, gp_far = exchange(
-        R, N, inputs_act, out_grad, pre_act, w_first, w_second
-    )
-    x_far = x_far.reshape(gp_far.shape[0], -1)
-    grad_first = (gf + contract_first(x_far, gp_far)) * factor
+    grad_input, gs, gf = exchange(R, N, inputs_act, out_grad, pre_act, w_first, w_second)
+    grad_first = gf.astype(jnp.float32) * factor
     grad_second = gs.astype(jnp.float32) * factor
     return (grad_input, grad_first, grad_second)
 

time: 203 us -> 193 us (0.951)
  matrix products: 8.7 us -> 0 us
  Pallas kernels: 188 us -> 180 us
  other arithmetic: 4.59 us -> 11.5 us
    dot_general x1 -> x0, matrix products: 8.7 us -> none  [contract_first(): lax.dot_general(left, right, (((0,), (0,)), ((), ())), preferred_element_...]
    pallas_call x1, Pallas kernels: 188 us -> 180 us  [exchange(): pl.pallas_call(functools.partial(kernel, R, N), out_shape=[jax.ShapeDtype...]
    mul x0 -> x1, other arithmetic: none -> 6.93 us  [on_device(): grad_first = gf.astype(jnp.float32) * factor]
where the time goes in v3:
time: 193 us
  Pallas kernels  180 us (93%)
  other arithmetic  11.5 us (6%)
    pallas_call x1, Pallas kernels, exchange(): pl.pallas_call(functools.partial(kernel, R, N), out_shape=[jax.ShapeDtype...  180 us
    mul x1, other arithmetic, on_device(): grad_first = gf.astype(jnp.float32) * factor  6.93 us
    mul x1, other arithmetic, on_device(): grad_second = gs.astype(jnp.float32) * factor  4.59 us

profile of v3, /device:TPU:7, one launch (start us, length us, event | category | flops | bytes accessed | tf_op | source)
XLA Modules:
  0.0 192.8 jit_solution(11999868639961891496)
XLA Ops:
  0.6 179.9 %shard_map.76 = (bf16[128,1024]{1,0:T(8,128)(2,1)}, bf16[2048,1024]{1,0:T(8,128)(2,1)}, bf16[1024,2048]{1,0:T(8,128)(2,1)}) custom-call(bf16[128,1024]{1,0:T(8,128)(2,1)} %x_ref.1, bf16[128,1024]{1,0:T(8,128)(2,1)} %dy_ref.1, bf16[256,2048]{1,0:T(8,128)(2,1)} %pre_ref.1, bf16[1024,2048]{1,0:T(8,128)(2,1)} %w1_ref.1, bf16[2048,1024]{1,0:T(8,128)(2,1)} %w2_ref.1), custom_call_target="tpu_custom_call" | custom-call | tf_op jit(solution)/shard_map/pallas_call | solution.py:438
  180.6 0.0 copy-start
  180.6 6.9 %convert_multiply_fusion.1 = f32[1024,2048]{1,0:T(8,128)} fusion(bf16[1024,2048]{1,0:T(8,128)(2,1)} %get-tuple-element.7), kind=kLoop, calls=%fused_computation.1 | loop fusion | flops 4194304 | bytes 12582912 | tf_op jit(solution)/shard_map/mul | solution.py:481
  187.5 0.0 copy-done
  187.5 0.0 copy-start.1
  187.5 4.6 %convert_multiply_fusion = f32[2048,1024]{1,0:T(8,128)} fusion(bf16[2048,1024]{1,0:T(8,128)(2,1)S(1)} %copy-done), kind=kLoop, calls=%fused_computation | loop fusion | flops 4194304 | bytes 12582912 | tf_op jit(solution)/shard_map/mul | solution.py:482
  192.1 0.0 copy-done.1
  192.1 0.7 copy.9
Async XLA Ops:
  180.6 6.9 %copy-start = (bf16[2048,1024]{1,0:T(8,128)(2,1)S(1)}, bf16[2048,1024]{1,0:T(8,128)(2,1)}, u32[]{:S(2)}) copy-start(bf16[2048,1024]{1,0:T(8,128)(2,1)} %get-tuple-element.8) | copy-start | bytes 12582916
  187.5 4.6 %copy-start.1 = (bf16[128,1024]{1,0:T(8,128)(2,1)S(1)}, bf16[128,1024]{1,0:T(8,128)(2,1)}, u32[]{:S(2)}) copy-start(bf16[128,1024]{1,0:T(8,128)(2,1)} %get-tuple-element.12) | copy-start | bytes 786436

commit v4 on v3

--- a/solution.py
+++ b/solution.py
@@ -61,6 +61,8 @@
     Tc, H = pre_ref.shape
     Dc = dy_ref.shape[1]
     part = Tc // SUB
+    FINE = 2 * SUB
+    fine = Tc // FINE
     last = N - 1
     f32, bf16 = jnp.float32, jnp.bfloat16
 
@@ -155,14 +157,14 @@
         return c <= k if side == 0 else last - c <= k
 
     def rs_copy(side, k, j):
-        rows = pl.ds(j * part, part)
+        rows = pl.ds(j * fine, fine)
         return pltpu.make_async_remote_copy(
             src_ref=hid.at[rs_shard(side, k), rows], dst_ref=rs.at[side, k, rows],
             send_sem=rs_s.at[side, k, j], recv_sem=rs_r.at[side, k, j],
             device_id={"col": sends_to(side)}, device_id_type=MESH)
 
     def rs_arrived(side, k, j):
-        rows = pl.ds(j * part, part)
+        rows = pl.ds(j * fine, fine)
         return pltpu.make_async_remote_copy(
             src_ref=hid.at[c, rows], dst_ref=rs.at[side, k, rows],
             send_sem=rs_s.at[side, k, j], recv_sem=rs_r.at[side, k, j],
@@ -213,12 +215,12 @@
         if s == last:
             @pl.when(c == 0)
             def _():
-                for j in range(SUB):
+                for j in range(FINE):
                     rs_copy(0, 0, j).start()
         if s == 0:
             @pl.when(c == last)
             def _():
-                for j in range(SUB):
+                for j in range(FINE):
                     rs_copy(1, 0, j).start()
 
     def act_block(s):
@@ -243,7 +245,7 @@
     pre_step(1)
     act_block(c)
     for k in range(1, last):
-        for j in range(SUB):
+        for j in range(FINE):
             for side in range(2):
                 edge = c == 0 if side == 0 else c == last
 
@@ -256,7 +258,7 @@
                         total = hid[s, rows, :].astype(f32) + rs[side, k - 1, rows, :].astype(f32)
                         hid[s, rows, :] = total.astype(bf16)
 
-                    strips(j * part, part, add)
+                    strips(j * fine, fine, add)
 
                 @pl.when(rs_sends(side, k))
                 def _():
@@ -281,7 +283,8 @@
         for side in range(2):
             @pl.when(c > 0 if side == 0 else c < last)
             def _():
-                rs_arrived(side, last - 1, j).wait_recv()
+                for piece in range(2 * j, 2 * j + 2):
+                    rs_arrived(side, last - 1, piece).wait_recv()
 
                 def add(rows):
                     acc[rows, :] = acc[rows, :] + rs[side, last - 1, rows, :].astype(f32)
@@ -422,7 +425,7 @@
 
         @pl.when(rs_sends(side, last - 1))
         def _():
-            for j in range(SUB):
+            for j in range(FINE):
                 rs_copy(side, last - 1, j).wait_send()
     for copy in (gs_copy, gf_copy):
         copy.wait()
@@ -464,7 +467,7 @@
             dma((2,)),
             dma((R // 2,)), dma((R,)), dma((R // 2,)), dma((R,)), dma((2, R // 2)),
             dma((2, N - 1)), dma((2, N - 1)),
-            dma((2, N - 1, SUB)), dma((2, N - 1, SUB)),
+            dma((2, N - 1, 2 * SUB)), dma((2, N - 1, 2 * SUB)),
             dma((2, N - 1, SUB)), dma((2, N - 1, SUB)),
             dma((R,)), dma((R,)),
         ],
@@ -474,12 +477,29 @@
     )(x, dy, pre, w1, w2)
 
 
+def widen(factor, *arrays):
+    steps = 8
+    specs = [pl.BlockSpec((a.shape[0] // steps, a.shape[1]), lambda i: (i, 0)) for a in arrays]
+
+    def body(a_ref, b_ref, a_out, b_out):
+        a_out[...] = a_ref[...].astype(jnp.float32) * factor
+        b_out[...] = b_ref[...].astype(jnp.float32) * factor
+
+    return pl.pallas_call(
+        body,
+        grid=(steps,),
+        in_specs=specs,
+        out_specs=specs,
+        out_shape=[jax.ShapeDtypeStruct(a.shape, jnp.float32) for a in arrays],
+        compiler_params=pltpu.CompilerParams(vmem_limit_bytes=60 * 2**20),
+    )(*arrays)
+
+
 def on_device(R, N, inputs_act, out_grad, pre_act, w_first, w_second):
     total_tokens = pre_act.shape[0] * N
     factor = 1.0 / math.sqrt(total_tokens)
     grad_input, gs, gf = exchange(R, N, inputs_act, out_grad, pre_act, w_first, w_second)
-    grad_first = gf.astype(jnp.float32) * factor
-    grad_second = gs.astype(jnp.float32) * factor
+    grad_first, grad_second = widen(factor, gf, gs)
     return (grad_input, grad_first, grad_second)
 
 

time: 193 us -> 192 us (level)
  other arithmetic: 11.5 us -> 0 us
  Pallas kernels: 180 us -> 190 us
    mul x2 -> x0, other arithmetic: 11.5 us -> none  [the longest x1 6.93 us: on_device(): grad_first = gf.astype(jnp.float32) * factor]
    pallas_call x0 -> x1, Pallas kernels: none -> 10.1 us  [widen(): pl.pallas_call(body, grid=(steps,), in_specs=specs, out_specs=specs, out_...]
where the time goes in v4:
time: 192 us
  Pallas kernels  190 us (99%)
    pallas_call x1, Pallas kernels, exchange(): pl.pallas_call(functools.partial(kernel, R, N), out_shape=[jax.ShapeDtype...  180 us
    pallas_call x1, Pallas kernels, widen(): pl.pallas_call(body, grid=(steps,), in_specs=specs, out_specs=specs, out_...  10.1 us

profile of v4, /device:TPU:7, one launch (start us, length us, event | category | flops | bytes accessed | tf_op | source)
XLA Modules:
  0.0 191.6 jit_solution(18198725002815089979)
XLA Ops:
  0.6 180.2 %shard_map.76 = (bf16[128,1024]{1,0:T(8,128)(2,1)}, bf16[2048,1024]{1,0:T(8,128)(2,1)}, bf16[1024,2048]{1,0:T(8,128)(2,1)}) custom-call(bf16[128,1024]{1,0:T(8,128)(2,1)} %x_ref.1, bf16[128,1024]{1,0:T(8,128)(2,1)} %dy_ref.1, bf16[256,2048]{1,0:T(8,128)(2,1)} %pre_ref.1, bf16[1024,2048]{1,0:T(8,128)(2,1)} %w1_ref.1, bf16[2048,1024]{1,0:T(8,128)(2,1)} %w2_ref.1), custom_call_target="tpu_custom_call" | custom-call | tf_op jit(solution)/shard_map/pallas_call | solution.py:441
  180.8 0.0 copy-start
  180.8 10.1 %shard_map.77 = (f32[1024,2048]{1,0:T(8,128)}, f32[2048,1024]{1,0:T(8,128)}) custom-call(bf16[1024,2048]{1,0:T(8,128)(2,1)} %get-tuple-element.9.a_ref, bf16[2048,1024]{1,0:T(8,128)(2,1)} %get-tuple-element.10.b_ref), custom_call_target="tpu_custom_call" | custom-call | tf_op jit(solution)/shard_map/pallas_call | solution.py:488
  190.9 0.0 copy-done
  190.9 0.7 copy.9
Async XLA Ops:
  180.8 10.1 %copy-start = (bf16[128,1024]{1,0:T(8,128)(2,1)S(1)}, bf16[128,1024]{1,0:T(8,128)(2,1)}, u32[]{:S(2)}) copy-start(bf16[128,1024]{1,0:T(8,128)(2,1)} %get-tuple-element.16) | copy-start | bytes 786436
